TPU v7x, 32 devices: a whole 2x2x4 slice. The times are simulated.
32 devices in a mesh: section: 8 (over z, x), sp: 4 (over y, core).
Axes of the slice: x: 2, y: 2, z: 4, core: 2. Of those that a mesh axis runs over, the one named last changes fastest.
Arguments:
- slots: bfloat16 [8, 64, 3072], P('section', 'sp'), may hold values from -6 to 6
- patch_of_slot: int32 [8], replicated, may hold values from 0 to 7, each once
- step_of_slot: int32 [8], replicated, may hold values from 0 to 26
- modulation: bfloat16 [8, 28, 3, 3072], P('section'), may hold values from -4 to 4
- w_qkv: bfloat16 [8, 3072, 3, 2048], P('section', None, None, 'sp'), may hold values from -0.109375 to 0.109375
- qk_scale: bfloat16 [8, 2, 128], P('section'), may hold values from 0.25 to 4
- w_mlp_in: bfloat16 [8, 3072, 6144], P('section', None, 'sp'), may hold values from -0.109375 to 0.109375
- w_attn_out: bfloat16 [8, 2048, 3072], P('section', 'sp'), may hold values from -0.125 to 0.125
- w_mlp_out: bfloat16 [8, 6144, 3072], P('section', 'sp'), may hold values from -0.078125 to 0.078125
- kv_cache: bfloat16 [8, 2, 512, 2048], P('section', None, None, 'sp'), may hold values from -130 to 130
Outputs:
- slots_out: bfloat16 [8, 64, 3072], P('section', 'sp')
- kv_cache_out: bfloat16 [8, 2, 512, 2048], P('section', None, None, 'sp')
Inputs may be any that keep to these rules, and one draw needn't show every extreme that they name: `patch_of_slot`: each patch id names exactly one slot.
All inputs are finite; a program needn't handle non-finite values.
Results may differ from a plain program's by a relative error of at most 0.012.
The roundings to bfloat16 on the way count: a program that leaves them out, or rounds other values in their place, can miss the bound.
Values may be sent and summed in bfloat16 or wider, within the bound.
A program may use at most 128 MiB of HBM per device.

v0:
```python
import math
import jax
import jax.numpy as jnp
from jax import lax
from jax.sharding import PartitionSpec as P

HD = 128
ROUNDS = 2


def shifted_2(x, axis, by):
    length = lax.axis_size(axis)
    return lax.ppermute(x, axis, [(i, (i + by) % length) for i in range(length)])


def slot_labels(patch_of_slot, step_of_slot, section_id, sections, round_id):
    anchor = section_id - round_id
    wrapped = (anchor < 0).astype(jnp.int32)
    anchor = anchor + wrapped * sections
    patch_id = lax.dynamic_index_in_dim(patch_of_slot, anchor, 0, keepdims=False)
    timestep = lax.dynamic_index_in_dim(step_of_slot, anchor, 0, keepdims=False) + wrapped
    return (patch_id, timestep)


def modulate(slot, table, timestep):
    factors = lax.dynamic_index_in_dim(table, timestep, 0, keepdims=False).astype(jnp.float32)
    wide = slot.astype(jnp.float32)
    center = wide - jnp.mean(wide, axis=-1, keepdims=True)
    spread = jnp.mean(center * center, axis=-1, keepdims=True)
    normed = (center * lax.rsqrt(spread + 1e-06) * (1.0 + factors[1]) + factors[0]).astype(
        jnp.bfloat16
    )
    return (normed, factors[2])


def head_norm(part, gain):
    rows = part.shape[0]
    wide = part.astype(jnp.float32).reshape(rows, -1, HD)
    power = jnp.mean(wide * wide, axis=-1, keepdims=True)
    normed = wide * lax.rsqrt(power + 1e-06) * gain.astype(jnp.float32)
    return normed.astype(jnp.bfloat16).reshape(rows, -1)


def mix(normed, patch_id, keys, values, qkv_weight, norm_gain, inner_weight):
    patch_rows = normed.shape[0]
    projected = jnp.einsum(
        "rd,dce->rce", normed, qkv_weight, preferred_element_type=jnp.float32
    ).astype(jnp.bfloat16)
    query_normed = head_norm(projected[:, 0], norm_gain[0])
    key_normed = head_norm(projected[:, 1], norm_gain[1])
    first_row = patch_id * patch_rows
    keys = lax.dynamic_update_slice_in_dim(keys, key_normed, first_row, 0)
    values = lax.dynamic_update_slice_in_dim(values, projected[:, 2], first_row, 0)
    local_heads = qkv_weight.shape[2] // HD
    queries = query_normed.reshape(patch_rows, local_heads, HD)
    key_heads = keys.reshape(keys.shape[0], local_heads, HD)
    value_heads = values.reshape(values.shape[0], local_heads, HD)
    scores = jnp.einsum(
        "rhd,thd->hrt", queries, key_heads, preferred_element_type=jnp.float32
    ) / math.sqrt(HD)
    shifted = jnp.exp(scores - jnp.max(scores, axis=-1, keepdims=True))
    weights = (shifted / jnp.sum(shifted, axis=-1, keepdims=True)).astype(jnp.bfloat16)
    attention = jnp.einsum(
        "hrt,thd->rhd", weights, value_heads, preferred_element_type=jnp.float32
    ).astype(jnp.bfloat16)
    attention = attention.reshape(patch_rows, local_heads * HD)
    activity = jax.nn.gelu(
        jnp.dot(normed, inner_weight, preferred_element_type=jnp.float32), approximate=True
    ).astype(jnp.bfloat16)
    return (attention, activity, keys, values)


def shards(
    slots,
    patch_of_slot,
    step_of_slot,
    modulation,
    w_qkv,
    qk_scale,
    w_mlp_in,
    w_attn_out,
    w_mlp_out,
    kv_cache,
):
    sections = lax.axis_size("section")
    section_id = lax.axis_index("section")
    table = modulation[0]
    qkv_weight = w_qkv[0]
    norm_gain = qk_scale[0]
    inner_weight = w_mlp_in[0]
    attention_weight = w_attn_out[0]
    outer_weight = w_mlp_out[0]
    keys = kv_cache[0, 0]
    values = kv_cache[0, 1]
    current = slots[0]
    for round_id in range(ROUNDS):
        patch_id, timestep = slot_labels(
            patch_of_slot, step_of_slot, section_id, sections, round_id
        )
        normed, gate = modulate(current, table, timestep)
        gathered = lax.all_gather(normed, "sp", axis=0, tiled=True)
        attention, activity, keys, values = mix(
            gathered, patch_id, keys, values, qkv_weight, norm_gain, inner_weight
        )
        summed = lax.psum_scatter(
            jnp.dot(attention, attention_weight, preferred_element_type=jnp.float32)
            + jnp.dot(activity, outer_weight, preferred_element_type=jnp.float32),
            "sp",
            scatter_dimension=0,
            tiled=True,
        )
        current = (current.astype(jnp.float32) + gate * summed).astype(jnp.bfloat16)
        current = shifted_2(current, "section", 1)
    return (current[None], jnp.stack([keys, values])[None])


def solution(mesh):
    return jax.shard_map(
        shards,
        mesh=mesh,
        in_specs=(
            P("section", "sp", None),
            P(),
            P(),
            P("section", None, None, None),
            P("section", None, None, "sp"),
            P("section", None, None),
            P("section", None, "sp"),
            P("section", "sp", None),
            P("section", "sp", None),
            P("section", None, None, "sp"),
        ),
        out_specs=(P("section", "sp", None), P("section", None, None, "sp")),
        check_vma=False,
    )
```

profile of v0, /device:TPU:0, one launch (start us, length us, event | category | flops | bytes accessed | tf_op | source)
XLA Modules:
  0.0 167.5 jit_solution(4243457292436387553)
XLA Ops:
  7.2 1.5 fusion.120
  14.3 8.0 %all_gather.6 = bf16[64,3072]{1,0:T(8,128)(2,1)S(1)} all-gather(bf16[16,3072]{1,0:T(8,128)(2,1)S(1)} %fusion.81), channel_id=1, replica_groups=mesh['section'=8,'sp'=4] {'sp'}, dimensions={0}, use_global_device_ids=true | all-gather | bytes 491520 | tf_op jit(solution)/shard_map/all_gather | solution.py:101
  23.0 5.4 %fusion.20 = bf16[64,3,512]{2,0,1:T(8,128)(2,1)S(1)} fusion(bf16[1,3072,3,512]{3,1,2,0:T(8,128)(2,1)} %param.14, bf16[64,3072]{1,0:T(8,128)(2,1)S(1)} %all_gather.6), kind=kOutput, calls=%fused_computation.24 | convolution fusion | flops 604078080 | bytes 10027008 | tf_op jit(solution)/shard_map/rd,dce->rce/dot_general | solution.py:46
  34.6 2.3 %slice_bitcast_fusion = (bf16[512,512]{1,0:T(8,128)(2,1)}, bf16[512,512]{1,0:T(8,128)(2,1)}) fusion(bf16[1,2,512,512]{3,2,1,0:T(8,128)(2,1)} %param.19), kind=kLoop, calls=%fused_computation.43 | loop fusion | bytes 2097152 | tf_op jit(solution)/shard_map/squeeze | solution.py:93
  39.6 1.3 fusion.99
  41.0 1.3 convolution_multiply_fusion.1
  43.3 2.0 %fusion.26 = bf16[4,8,8,128]{3,2,1,0:T(8,128)(2,1)S(1)} fusion(f32[4,64]{1,0:T(4,128)S(1)} %fusion.122, f32[4,64,512]{2,1,0:T(8,128)} %copy-done.3, bf16[512,512]{1,0:T(8,128)(2,1)} %get-tuple-element.9), kind=kOutput, calls=%fused_computation.28 | convolution fusion | flops 33981184 | bytes 1115136 | tf_op jit(solution)/shard_map/hrt,thd->rhd/dot_general | solution.py:63
  45.4 10.8 %fusion.4 = f32[64,3072]{1,0:T(8,128)} fusion(bf16[1,1536,3072]{2,1,0:T(8,128)(2,1)} %param.18, bf16[64,3072]{1,0:T(8,128)(2,1)} %copy-done.1, bf16[1,3072,1536]{2,1,0:T(8,128)(2,1)} %param.16), kind=kOutput, calls=%fused_computation.4 | convolution fusion | flops 1208844288 | bytes 20054016 | tf_op jit(solution)/shard_map/dot_general | solution.py:107
  56.2 2.7 %convolution_add_fusion.1 = f32[64,3072]{1,0:T(8,128)} fusion(f32[64,3072]{1,0:T(8,128)} %fusion.4, bf16[1,512,3072]{2,1,0:T(8,128)(2,1)S(1)} %copy-done, bf16[4,8,8,128]{3,2,1,0:T(8,128)(2,1)S(1)} %fusion.26), kind=kOutput, calls=%fused_computation.15 | convolution fusion | flops 201523200 | bytes 4784128 | tf_op jit(solution)/shard_map/dot_general | solution.py:106
  58.9 24.2 %reduce-scatter.3.cloned.1.call-done = f32[16,3072]{1,0:T(8,128)} async-done(((f32[64,3072]{1,0:T(8,128)}), f32[16,3072]{1,0:T(8,128)}) %reduce-scatter.3.cloned.1.call-update) | async-done | bytes 196624 | tf_op jit(solution)/shard_map/reduce_scatter | solution.py:105
  84.1 1.5 collective-permute-start
  86.3 5.2 %collective-permute-done = bf16[16,3072]{1,0:T(8,128)(2,1)S(1)} collective-permute-done((bf16[16,3072]{1,0:T(8,128)(2,1)S(1)}, bf16[16,3072]{1,0:T(8,128)(2,1)S(1)}, u32[]{:S(2)}, u32[]{:S(2)}) %collective-permute-start) | collective-permute-done | bytes 98336 | tf_op jit(solution)/shard_map/ppermute | solution.py:13
  92.0 6.3 %all_gather.7 = bf16[64,3072]{1,0:T(8,128)(2,1)S(1)} all-gather(bf16[16,3072]{1,0:T(8,128)(2,1)S(1)} %fusion.77), channel_id=1, replica_groups=mesh['section'=8,'sp'=4] {'sp'}, dimensions={0}, use_global_device_ids=true | all-gather | bytes 491520 | tf_op jit(solution)/shard_map/all_gather | solution.py:101
  99.0 5.4 %fusion.23 = bf16[64,3,512]{2,0,1:T(8,128)(2,1)S(1)} fusion(bf16[1,3072,3,512]{3,1,2,0:T(8,128)(2,1)} %param.14, bf16[64,3072]{1,0:T(8,128)(2,1)S(1)} %all_gather.7), kind=kOutput, calls=%fused_computation.25 | convolution fusion | flops 604078080 | bytes 10027008 | tf_op jit(solution)/shard_map/rd,dce->rce/dot_general | solution.py:46
  105.8 10.8 %fusion.2 = f32[64,3072]{1,0:T(8,128)} fusion(bf16[1,1536,3072]{2,1,0:T(8,128)(2,1)} %param.18, bf16[64,3072]{1,0:T(8,128)(2,1)} %copy-done.2, bf16[1,3072,1536]{2,1,0:T(8,128)(2,1)} %param.16), kind=kOutput, calls=%fused_computation.2 | convolution fusion | flops 1208844288 | bytes 20054016 | tf_op jit(solution)/shard_map/dot_general | solution.py:107
  116.5 1.6 mul.270
  119.2 1.6 reshape.151
  123.7 1.3 convolution_multiply_fusion
  126.1 1.9 %fusion.27 = bf16[4,8,8,128]{3,2,1,0:T(8,128)(2,1)S(1)} fusion(f32[4,64]{1,0:T(4,128)S(1)} %fusion.123, f32[4,64,512]{2,1,0:T(8,128)} %copy-done.4, bf16[512,512]{1,0:T(8,128)(2,1)} %get-tuple-element.7), kind=kOutput, calls=%fused_computation.29 | convolution fusion | flops 33981184 | bytes 1115136 | tf_op jit(solution)/shard_map/hrt,thd->rhd/dot_general | solution.py:63
  128.1 2.7 %convolution_add_fusion = f32[64,3072]{1,0:T(8,128)} fusion(f32[64,3072]{1,0:T(8,128)} %fusion.2, bf16[1,512,3072]{2,1,0:T(8,128)(2,1)S(1)} %copy-done, bf16[4,8,8,128]{3,2,1,0:T(8,128)(2,1)S(1)} %fusion.27), kind=kOutput, calls=%fused_computation.14 | convolution fusion | flops 201523200 | bytes 4784128 | tf_op jit(solution)/shard_map/dot_general | solution.py:106
  130.8 21.0 %reduce-scatter.5.cloned.1.call-done = f32[16,3072]{1,0:T(8,128)} async-done(((f32[64,3072]{1,0:T(8,128)}), f32[16,3072]{1,0:T(8,128)}) %reduce-scatter.5.cloned.1.call-update) | async-done | bytes 196624 | tf_op jit(solution)/shard_map/reduce_scatter | solution.py:105
  152.7 1.5 collective-permute-start.1
  154.2 2.3 %maximum_bitcast_fusion = bf16[1,2,512,512]{3,2,1,0:T(8,128)(2,1)} fusion(bf16[1,512,512]{2,1,0:T(8,128)(2,1)} %bitcast.182, bf16[1,512,512]{2,1,0:T(8,128)(2,1)} %bitcast.181), kind=kLoop, calls=%fused_computation.30 | loop fusion | flops 524288 | bytes 2097152 | tf_op jit(solution)/shard_map/broadcast_in_dim | solution.py:114
  156.5 3.6 %collective-permute-done.1 = bf16[16,3072]{1,0:T(8,128)(2,1)S(1)} collective-permute-done((bf16[16,3072]{1,0:T(8,128)(2,1)S(1)}, bf16[16,3072]{1,0:T(8,128)(2,1)S(1)}, u32[]{:S(2)}, u32[]{:S(2)}) %collective-permute-start.1) | collective-permute-done | bytes 98336 | tf_op jit(solution)/shard_map/ppermute | solution.py:13
  (59 shorter events, 24.6 us)
Async XLA Ops:
  7.2 49.0 %copy-start = (bf16[1,512,3072]{2,1,0:T(8,128)(2,1)S(1)}, bf16[1,512,3072]{2,1,0:T(8,128)(2,1)}, u32[]{:S(2)}) copy-start(bf16[1,512,3072]{2,1,0:T(8,128)(2,1)} %param.17) | copy-start | bytes 9437188
  7.2 76.0 %reduce-scatter.3.cloned.1.call-start = ((), (), s32[]{:S(2)}) async-start(), calls=%async_computation.2 | async-start | bytes 983040 | tf_op jit(solution)/shard_map/reduce_scatter | solution.py:105
  22.2 0.7 copy-start.1
  42.3 0.8 copy-start.3
  45.4 37.8 %copy-start.5 = (bf16[1,16,3072]{2,1,0:T(8,128)(2,1)S(1)}, bf16[1,16,3072]{2,1,0:T(8,128)(2,1)}, u32[]{:S(2)}) copy-start(bf16[1,16,3072]{2,1,0:T(8,128)(2,1)} %param.10) | copy-start | bytes 294916
  58.9 92.9 %reduce-scatter.5.cloned.1.call-start = ((), (), s32[]{:S(2)}) async-start(), calls=%async_computation.3 | async-start | bytes 983040 | tf_op jit(solution)/shard_map/reduce_scatter | solution.py:105
  84.1 7.4 %collective-permute-start = (bf16[16,3072]{1,0:T(8,128)(2,1)S(1)}, bf16[16,3072]{1,0:T(8,128)(2,1)S(1)}, u32[]{:S(2)}, u32[]{:S(2)}) collective-permute-start(bf16[16,3072]{1,0:T(8,128)(2,1)S(1)} %fusion.82), channel_id=1, source_target_pairs={{0,4},{4,8},{8,12},{12,16},{16,20},{20,24},{24,28},{28,0},{1,5},{5... | collective-permute-start | bytes 294920 | tf_op jit(solution)/shard_map/ppermute | solution.py:13
  98.3 0.7 copy-start.2
  105.8 16.1 %copy-start.7 = (f32[128]{0:T(128)S(1)}, f32[128]{0:T(128)}, u32[]{:S(2)}) copy-start(f32[128]{0:T(128)} %get-tuple-element.20) | copy-start | bytes 1540
  105.8 17.3 %copy-start.6 = (f32[512]{0:T(512)S(1)}, f32[512]{0:T(512)}, u32[]{:S(2)}) copy-start(f32[512]{0:T(512)} %broadcast_bitcast_fusion) | copy-start | bytes 6148
  125.1 0.8 copy-start.4
  152.7 7.4 %collective-permute-start.1 = (bf16[16,3072]{1,0:T(8,128)(2,1)S(1)}, bf16[16,3072]{1,0:T(8,128)(2,1)S(1)}, u32[]{:S(2)}, u32[]{:S(2)}) collective-permute-start(bf16[16,3072]{1,0:T(8,128)(2,1)S(1)} %fusion.83), channel_id=1, source_target_pairs={{0,4},{4,8},{8,12},{12,16},{16,20},{20,24},{24,28},{28,0},{1,5},{5... | collective-permute-start | bytes 294920 | tf_op jit(solution)/shard_map/ppermute | solution.py:13
Sparse Core Ops, SparseCore 0:
  59.0 24.1 reduce-scatter.2
  130.9 20.7 reduce-scatter.4
where the time goes:
time: 169 us; the launch traced here: 168 us
  waiting for transfers between devices  54 us (32%)
  matrix products  44.3 us (26%)
  other arithmetic  21.6 us (13%)
  between operations  16.8 us (10%)
  blocking collectives  14.3 us (8%)
  local copies, waits for them, and re-layouts  13.4 us (8%)
  starting transfers between devices  3.15 us (2%)
    reduce_scatter x2, waiting for transfers between devices, shards(): lax.psum_scatter(jnp.dot(attention, attention_weight, preferred_element_t...  45.2 us
    dot_general x2, matrix products, shards(): jnp.dot(activity, outer_weight, preferred_element_type=jnp.float32)  21.6 us
    all_gather x2, blocking collectives, shards(): gathered = lax.all_gather(normed, 'sp', axis=0, tiled=True)  14.3 us
    dot_general x2, matrix products, mix(): jnp.einsum('rd,dce->rce', normed, qkv_weight, preferred_element_type=jnp....  10.8 us
    ppermute x2, waiting for transfers between devices, shifted_2(): lax.ppermute(x, axis, [(i, (i + by) % length) for i in range(length)])  8.74 us
    dot_general x2, matrix products, shards(): jnp.dot(attention, attention_weight, preferred_element_type=jnp.float32)  5.36 us
    dot_general x2, matrix products, mix(): jnp.einsum('hrt,thd->rhd', weights, value_heads, preferred_element_type=j...  3.95 us
    unnamed x17, local copies, waits for them, and re-layouts  3.75 us
  transfers between devices with their start and end apart: 4, of which 4 were waited for; matrix products, arithmetic and copies ran while one was open for 1% of the time, Pallas kernels for 0%

commit v1 on v0

--- a/solution.py
+++ b/solution.py
@@ -6,6 +6,18 @@
 
 HD = 128
 ROUNDS = 2
+
+
+def collect(shard, axis, dim):
+    ways, here = (lax.axis_size(axis), lax.axis_index(axis))
+    grown, reach = (shard, 1)
+    while reach < ways:
+        theirs = lax.ppermute(grown, axis, [(d, d ^ reach) for d in range(ways)])
+        mine_first = jnp.concatenate([grown, theirs], axis=dim)
+        theirs_first = jnp.concatenate([theirs, grown], axis=dim)
+        grown = jnp.where(here & reach == 0, mine_first, theirs_first)
+        reach = 2 * reach
+    return grown
 
 
 def shifted_2(x, axis, by):
@@ -98,7 +110,7 @@
             patch_of_slot, step_of_slot, section_id, sections, round_id
         )
         normed, gate = modulate(current, table, timestep)
-        gathered = lax.all_gather(normed, "sp", axis=0, tiled=True)
+        gathered = collect(normed, "sp", 0)
         attention, activity, keys, values = mix(
             gathered, patch_id, keys, values, qkv_weight, norm_gain, inner_weight
         )

time: 169 us -> 179 us (1.059)
  blocking collectives: 14.3 us -> 0 us
  waiting for transfers between devices: 54 us -> 67.2 us
  other arithmetic: 21.6 us -> 25.5 us
  starting transfers between devices: 3.15 us -> 6.92 us
  local copies, waits for them, and re-layouts: 13.4 us -> 15.6 us
    all_gather x2 -> x0, blocking collectives: 14.3 us -> none  [shards(): gathered = lax.all_gather(normed, 'sp', axis=0, tiled=True)]
    ppermute x0 -> x4, waiting for transfers between devices: none -> 12.2 us  [collect(): theirs = lax.ppermute(grown, axis, [(d, d ^ reach) for d in range(ways)])]
    ppermute x0 -> x4, starting transfers between devices: none -> 3.62 us  [collect(): theirs = lax.ppermute(grown, axis, [(d, d ^ reach) for d in range(ways)])]
    reduce_sum x4, other arithmetic: 2.98 us -> 5.4 us  [head_norm(): power = jnp.mean(wide * wide, axis=-1, keepdims=True)]
  transfers between devices with their start and end apart: 4 -> 8, of which waited for: 4 -> 7; matrix products, arithmetic and copies ran while one was open for 1% -> 4% of each run, Pallas kernels for 0% -> 0%
where the time goes in v1:
time: 179 us; the launch traced here: 178 us
  waiting for transfers between devices  67.2 us (38%)
  matrix products  45.6 us (25%)
  other arithmetic  25.5 us (14%)
  between operations  16.9 us (9%)
  local copies, waits for them, and re-layouts  15.6 us (9%)
  starting transfers between devices  6.92 us (4%)
    reduce_scatter x2, waiting for transfers between devices, shards(): lax.psum_scatter(jnp.dot(attention, attention_weight, preferred_element_t...  45.5 us
    dot_general x2, matrix products, shards(): jnp.dot(activity, outer_weight, preferred_element_type=jnp.float32)  21.9 us
    ppermute x4, waiting for transfers between devices, collect(): theirs = lax.ppermute(grown, axis, [(d, d ^ reach) for d in range(ways)])  12.2 us
    dot_general x2, matrix products, mix(): jnp.einsum('rd,dce->rce', normed, qkv_weight, preferred_element_type=jnp....  11 us
    ppermute x2, waiting for transfers between devices, shifted_2(): lax.ppermute(x, axis, [(i, (i + by) % length) for i in range(length)])  9.4 us
    reduce_sum x4, other arithmetic, head_norm(): power = jnp.mean(wide * wide, axis=-1, keepdims=True)  5.4 us
    dot_general x2, matrix products, shards(): jnp.dot(attention, attention_weight, preferred_element_type=jnp.float32)  5.39 us
    dot_general x2, matrix products, mix(): jnp.einsum('hrt,thd->rhd', weights, value_heads, preferred_element_type=j...  4.63 us
  transfers between devices with their start and end apart: 8, of which 7 were waited for; matrix products, arithmetic and copies ran while one was open for 4% of the time, Pallas kernels for 0%

profile of v1, /device:TPU:0, one launch (start us, length us, event | category | flops | bytes accessed | tf_op | source)
XLA Modules:
  0.0 177.6 jit_solution(1312130314269125636)
XLA Ops:
  10.1 1.7 dynamic-slice_convert_fusion
  15.5 2.3 %slice_bitcast_fusion = (bf16[512,512]{1,0:T(8,128)(2,1)}, bf16[512,512]{1,0:T(8,128)(2,1)}) fusion(bf16[1,2,512,512]{3,2,1,0:T(8,128)(2,1)} %param.19), kind=kLoop, calls=%fused_computation.43 | loop fusion | bytes 2097152 | tf_op jit(solution)/shard_map/squeeze | solution.py:105
  19.7 2.6 %collective-permute-start.1 = (bf16[32,3072]{1,0:T(8,128)(2,1)S(1)}, bf16[32,3072]{1,0:T(8,128)(2,1)S(1)}, u32[]{:S(2)}, u32[]{:S(2)}) collective-permute-start(bf16[32,3072]{1,0:T(8,128)(2,1)S(1)} %maximum_select_fusion.2), channel_id=1, source_target_pairs={{0,2},{1,3},{2,0},{3,1},{4,6},{5,7},{6,4},{7,5},{8,10},{9,11},{10,... | collective-permute-start | bytes 589832 | tf_op jit(solution)/shard_map/ppermute | solution.py:15
  23.0 4.9 %collective-permute-done.1 = bf16[32,3072]{1,0:T(8,128)(2,1)S(1)} collective-permute-done((bf16[32,3072]{1,0:T(8,128)(2,1)S(1)}, bf16[32,3072]{1,0:T(8,128)(2,1)S(1)}, u32[]{:S(2)}, u32[]{:S(2)}) %collective-permute-start.1) | collective-permute-done | bytes 196640 | tf_op jit(solution)/shard_map/ppermute | solution.py:15
  28.6 5.4 %fusion.20 = bf16[64,3,512]{2,0,1:T(8,128)(2,1)S(1)} fusion(bf16[1,3072,3,512]{3,1,2,0:T(8,128)(2,1)} %param.14, bf16[32,3072]{1,0:T(8,128)(2,1)S(1)} %collective-permute-done.1, bf16[32,3072]{1,0:T(8,128)(2,1)S(1)} %maximum_select_fusion.2, pred[]{:T(512)S(6)} %eq.8), kind=kOutput, calls=%fused_computation.24 | convolution fusion | flops 605847552 | bytes 10027009 | tf_op jit(solution)/shard_map/rd,dce->rce/dot_general | solution.py:58
  35.3 1.6 mul.239
  36.9 1.7 reduce_sum.93
  39.9 1.6 reshape.147
  47.6 2.6 %fusion.26 = bf16[4,8,8,128]{3,2,1,0:T(8,128)(2,1)} fusion(f32[4,64]{1,0:T(4,128)S(1)} %fusion.128, f32[4,64,512]{2,1,0:T(8,128)} %copy-done.1, bf16[512,512]{1,0:T(8,128)(2,1)} %get-tuple-element.9), kind=kOutput, calls=%fused_computation.28 | convolution fusion | flops 33981184 | bytes 1115136 | tf_op jit(solution)/shard_map/hrt,thd->rhd/dot_general | solution.py:75
  50.2 10.9 %fusion.4 = f32[64,3072]{1,0:T(8,128)} fusion(bf16[1,1536,3072]{2,1,0:T(8,128)(2,1)} %param.18, bf16[1,3072,1536]{2,1,0:T(8,128)(2,1)} %param.16, bf16[32,3072]{1,0:T(8,128)(2,1)} %copy-done.6, bf16[32,3072]{1,0:T(8,128)(2,1)S(1)} %maximum_select_fusion.2, pred[]{:T(512)S(6)} %eq.8), kind=kOutput, calls=%fused_computation.4 | convolution fusion | flops 1210613760 | bytes 20054016 | tf_op jit(solution)/shard_map/dot_general | solution.py:119
  61.1 2.7 %convolution_add_fusion.1 = f32[64,3072]{1,0:T(8,128)} fusion(f32[64,3072]{1,0:T(8,128)} %fusion.4, bf16[1,512,3072]{2,1,0:T(8,128)(2,1)S(1)} %copy-done, bf16[4,8,8,128]{3,2,1,0:T(8,128)(2,1)} %fusion.26), kind=kOutput, calls=%fused_computation.15 | convolution fusion | flops 201523200 | bytes 4784128 | tf_op jit(solution)/shard_map/dot_general | solution.py:118
  63.9 24.8 %reduce-scatter.3.cloned.1.call-done = f32[16,3072]{1,0:T(8,128)} async-done(((f32[64,3072]{1,0:T(8,128)}), f32[16,3072]{1,0:T(8,128)}) %reduce-scatter.3.cloned.1.call-update) | async-done | bytes 196624 | tf_op jit(solution)/shard_map/reduce_scatter | solution.py:117
  89.7 1.7 collective-permute-start.2
  91.4 5.8 %collective-permute-done.2 = bf16[16,3072]{1,0:T(8,128)(2,1)S(1)} collective-permute-done((bf16[16,3072]{1,0:T(8,128)(2,1)S(1)}, bf16[16,3072]{1,0:T(8,128)(2,1)S(1)}, u32[]{:S(2)}, u32[]{:S(2)}) %collective-permute-start.2) | collective-permute-done | bytes 98336 | tf_op jit(solution)/shard_map/ppermute | solution.py:25
  100.1 6.1 %collective-permute-done.4 = bf16[32,3072]{1,0:T(8,128)(2,1)} collective-permute-done((bf16[32,3072]{1,0:T(8,128)(2,1)S(1)}, bf16[32,3072]{1,0:T(8,128)(2,1)}, u32[]{:S(2)}, u32[]{:S(2)}) %collective-permute-start.4) | collective-permute-done | bytes 196640 | tf_op jit(solution)/shard_map/ppermute | solution.py:15
  106.2 5.6 %fusion.23 = bf16[64,3,512]{2,0,1:T(8,128)(2,1)S(1)} fusion(bf16[1,3072,3,512]{3,1,2,0:T(8,128)(2,1)} %param.14, bf16[32,3072]{1,0:T(8,128)(2,1)} %collective-permute-done.4, bf16[32,3072]{1,0:T(8,128)(2,1)S(1)} %maximum_select_fusion.3, pred[]{:T(512)S(6)} %eq.8), kind=kOutput, calls=%fused_computation.25 | convolution fusion | flops 605847552 | bytes 10027009 | tf_op jit(solution)/shard_map/rd,dce->rce/dot_general | solution.py:58
  113.2 1.6 mul.270
  114.8 1.6 reduce_sum.98
  125.4 2.0 %fusion.27 = bf16[4,8,8,128]{3,2,1,0:T(8,128)(2,1)S(1)} fusion(f32[4,64]{1,0:T(4,128)S(1)} %fusion.129, f32[4,64,512]{2,1,0:T(8,128)} %copy-done.2, bf16[512,512]{1,0:T(8,128)(2,1)} %get-tuple-element.7), kind=kOutput, calls=%fused_computation.29 | convolution fusion | flops 33981184 | bytes 1115136 | tf_op jit(solution)/shard_map/hrt,thd->rhd/dot_general | solution.py:75
  127.5 10.9 %fusion.2 = f32[64,3072]{1,0:T(8,128)} fusion(bf16[1,1536,3072]{2,1,0:T(8,128)(2,1)} %param.18, bf16[1,3072,1536]{2,1,0:T(8,128)(2,1)} %param.16, bf16[32,3072]{1,0:T(8,128)(2,1)} %collective-permute-done.4, bf16[32,3072]{1,0:T(8,128)(2,1)S(1)} %maximum_select_fusion.3, pred[]{:T(512)S(6)} %eq.8), kind=kOutput, calls=%fused_computation.2 | convolution fusion | flops 1210613760 | bytes 20054016 | tf_op jit(solution)/shard_map/dot_general | solution.py:119
  138.4 2.7 %convolution_add_fusion = f32[64,3072]{1,0:T(8,128)} fusion(f32[64,3072]{1,0:T(8,128)} %fusion.2, bf16[1,512,3072]{2,1,0:T(8,128)(2,1)S(1)} %copy-done, bf16[4,8,8,128]{3,2,1,0:T(8,128)(2,1)S(1)} %fusion.27), kind=kOutput, calls=%fused_computation.14 | convolution fusion | flops 201523200 | bytes 4784128 | tf_op jit(solution)/shard_map/dot_general | solution.py:118
  141.1 20.7 %reduce-scatter.5.cloned.1.call-done = f32[16,3072]{1,0:T(8,128)} async-done(((f32[64,3072]{1,0:T(8,128)}), f32[16,3072]{1,0:T(8,128)}) %reduce-scatter.5.cloned.1.call-update) | async-done | bytes 196624 | tf_op jit(solution)/shard_map/reduce_scatter | solution.py:117
  164.3 2.3 %maximum_bitcast_fusion = bf16[1,2,512,512]{3,2,1,0:T(8,128)(2,1)} fusion(bf16[1,512,512]{2,1,0:T(8,128)(2,1)} %bitcast.180, bf16[1,512,512]{2,1,0:T(8,128)(2,1)} %bitcast.179), kind=kLoop, calls=%fused_computation.30 | loop fusion | flops 524288 | bytes 2097152 | tf_op jit(solution)/shard_map/broadcast_in_dim | solution.py:126
  166.5 3.6 %collective-permute-done.5 = bf16[16,3072]{1,0:T(8,128)(2,1)S(1)} collective-permute-done((bf16[16,3072]{1,0:T(8,128)(2,1)S(1)}, bf16[16,3072]{1,0:T(8,128)(2,1)S(1)}, u32[]{:S(2)}, u32[]{:S(2)}) %collective-permute-start.5) | collective-permute-done | bytes 98336 | tf_op jit(solution)/shard_map/ppermute | solution.py:25
  (67 shorter events, 33.4 us)
Async XLA Ops:
  7.2 54.0 %copy-start = (bf16[1,512,3072]{2,1,0:T(8,128)(2,1)S(1)}, bf16[1,512,3072]{2,1,0:T(8,128)(2,1)}, u32[]{:S(2)}) copy-start(bf16[1,512,3072]{2,1,0:T(8,128)(2,1)} %param.17) | copy-start | bytes 9437188
  7.2 81.5 %reduce-scatter.3.cloned.1.call-start = ((), (), s32[]{:S(2)}) async-start(), calls=%async_computation.2 | async-start | bytes 983040 | tf_op jit(solution)/shard_map/reduce_scatter | solution.py:117
  15.0 4.7 %collective-permute-start = (bf16[16,3072]{1,0:T(8,128)(2,1)S(1)}, bf16[16,3072]{1,0:T(8,128)(2,1)S(1)}, u32[]{:S(2)}, u32[]{:S(2)}) collective-permute-start(bf16[16,3072]{1,0:T(8,128)(2,1)S(1)} %fusion.81), channel_id=1, source_target_pairs={{0,1},{1,0},{2,3},{3,2},{4,5},{5,4},{6,7},{7,6},{8,9},{9,8},{10,11... | collective-permute-start | bytes 294920 | tf_op jit(solution)/shard_map/ppermute | solution.py:15
  19.7 8.1 %collective-permute-start.1 = (bf16[32,3072]{1,0:T(8,128)(2,1)S(1)}, bf16[32,3072]{1,0:T(8,128)(2,1)S(1)}, u32[]{:S(2)}, u32[]{:S(2)}) collective-permute-start(bf16[32,3072]{1,0:T(8,128)(2,1)S(1)} %maximum_select_fusion.2), channel_id=1, source_target_pairs={{0,2},{1,3},{2,0},{3,1},{4,6},{5,7},{6,4},{7,5},{8,10},{9,11},{10,... | collective-permute-start | bytes 589832 | tf_op jit(solution)/shard_map/ppermute | solution.py:15
  27.9 0.7 copy-start.6
  46.5 0.8 copy-start.1
  50.2 38.5 %copy-start.3 = (bf16[1,16,3072]{2,1,0:T(8,128)(2,1)S(1)}, bf16[1,16,3072]{2,1,0:T(8,128)(2,1)}, u32[]{:S(2)}) copy-start(bf16[1,16,3072]{2,1,0:T(8,128)(2,1)} %param.10) | copy-start | bytes 294916
  50.2 41.2 %copy-start.7 = (f32[1,1,3,3072]{3,1,2,0:T(1,128)S(1)}, f32[1,1,3,3072]{3,1,2,0:T(1,128)}, u32[]{:S(2)}) copy-start(f32[1,1,3,3072]{3,1,2,0:T(1,128)} %get-tuple-element.4) | copy-start | bytes 110596
  63.9 97.9 %reduce-scatter.5.cloned.1.call-start = ((), (), s32[]{:S(2)}) async-start(), calls=%async_computation.3 | async-start | bytes 983040 | tf_op jit(solution)/shard_map/reduce_scatter | solution.py:117
  89.7 7.5 %collective-permute-start.2 = (bf16[16,3072]{1,0:T(8,128)(2,1)S(1)}, bf16[16,3072]{1,0:T(8,128)(2,1)S(1)}, u32[]{:S(2)}, u32[]{:S(2)}) collective-permute-start(bf16[16,3072]{1,0:T(8,128)(2,1)S(1)} %fusion.82), channel_id=1, source_target_pairs={{0,4},{4,8},{8,12},{12,16},{16,20},{20,24},{24,28},{28,0},{1,5},{5... | collective-permute-start | bytes 294920 | tf_op jit(solution)/shard_map/ppermute | solution.py:25
  97.2 0.6 copy-start.4
  97.7 1.4 collective-permute-start.3
  99.1 7.1 %collective-permute-start.4 = (bf16[32,3072]{1,0:T(8,128)(2,1)S(1)}, bf16[32,3072]{1,0:T(8,128)(2,1)}, u32[]{:S(2)}, u32[]{:S(2)}) collective-permute-start(bf16[32,3072]{1,0:T(8,128)(2,1)S(1)} %maximum_select_fusion.3), channel_id=1, source_target_pairs={{0,2},{1,3},{2,0},{3,1},{4,6},{5,7},{6,4},{7,5},{8,10},{9,11},{10,... | collective-permute-start | bytes 589832 | tf_op jit(solution)/shard_map/ppermute | solution.py:15
  124.4 0.8 copy-start.2
  127.5 34.4 %copy-start.5 = (bf16[16,3072]{1,0:T(8,128)(2,1)S(1)}, bf16[16,3072]{1,0:T(8,128)(2,1)}, u32[]{:S(2)}) copy-start(bf16[16,3072]{1,0:T(8,128)(2,1)} %copy-done.4) | copy-start | bytes 294916
  162.8 7.4 %collective-permute-start.5 = (bf16[16,3072]{1,0:T(8,128)(2,1)S(1)}, bf16[16,3072]{1,0:T(8,128)(2,1)S(1)}, u32[]{:S(2)}, u32[]{:S(2)}) collective-permute-start(bf16[16,3072]{1,0:T(8,128)(2,1)S(1)} %fusion.83), channel_id=1, source_target_pairs={{0,4},{4,8},{8,12},{12,16},{16,20},{20,24},{24,28},{28,0},{1,5},{5... | collective-permute-start | bytes 294920 | tf_op jit(solution)/shard_map/ppermute | solution.py:25
Sparse Core Ops, SparseCore 0:
  64.0 24.6 reduce-scatter.2
  141.2 20.5 reduce-scatter.4
